TPU v7x, 32 devices: a whole 2x2x4 slice. The times are simulated.
32 devices in a mesh: rows: 2 (over x), feat: 16 (over z, y, core).
Axes of the slice: x: 2, y: 2, z: 4, core: 2. Of those that a mesh axis runs over, the one named last changes fastest.
Arguments:
- slab_grads: bfloat16 [448, 262144], P('rows', 'feat'), may hold values from -6 to 6
- basis: bfloat16 [262144, 1024], P('feat', 'rows'), may hold values from -0.01171875 to 0.01171875
- eigenvalues: float32 [1024], replicated, may hold values from 0.02 to 2
- store_rows: bfloat16 [16384, 1024], P(('rows', 'feat')), may hold values from -0.1875 to 0.1875
- slab_index: int32 [448], replicated, may hold values from 0 to 16383
Outputs:
- scores: float32 [448, 16384], P(None, ('rows', 'feat'))
All inputs are finite; a program needn't handle non-finite values.
Results may differ from a plain program's by a relative error of at most 0.0029.
Values may be sent and summed in bfloat16 or wider, within the bound.
No kernel may reach another device: no remote copies, remote signals or barrier semaphores. Data moves between devices by JAX's collectives and lax.ppermute only.
A program may use at most 128 MiB of HBM per device.

v0:
```python
import jax
import jax.numpy as jnp
from jax import lax
from jax.sharding import PartitionSpec as P

DAMPING = 0.1


def shards(slab_grads, basis, eigenvalues, store_rows, slab_index):
    feat_groups = lax.axis_size("feat")
    store_count = store_rows.shape[0]
    first_column = (lax.axis_index("rows") * feat_groups + lax.axis_index("feat")) * store_count
    columns = first_column + jnp.arange(store_count, dtype=jnp.int32)
    local_dirs = basis.shape[1]
    partial_value = jnp.dot(
        lax.all_gather(slab_grads, "rows", axis=0, tiled=True),
        basis,
        preferred_element_type=jnp.float32,
    )
    summed = lax.psum(partial_value, "feat")
    scales = lax.dynamic_slice_in_dim(
        eigenvalues, lax.axis_index("rows") * local_dirs, local_dirs, 0
    )
    whitened = (summed / (scales + DAMPING)).astype(jnp.bfloat16)
    gathered = lax.all_gather(whitened, "rows", axis=1, tiled=True)
    product = lax.dot_general(
        gathered, store_rows, (((1,), (1,)), ((), ())), preferred_element_type=jnp.float32
    )
    return jnp.where(slab_index[:, None] == columns[None, :], jnp.zeros_like(product), product)


def solution(mesh):
    in_specs = (P("rows", "feat"), P("feat", "rows"), P(), P(("rows", "feat"), None), P())
    out_specs = P(None, ("rows", "feat"))
    return jax.shard_map(shards, mesh=mesh, in_specs=in_specs, out_specs=out_specs, check_vma=False)
```

profile of v0, /device:TPU:0, one launch (start us, length us, event | category | flops | bytes accessed | tf_op | source)
XLA Modules:
  0.0 319.1 jit_solution(506024882513834059)
XLA Ops:
  6.5 0.0 copy-start
  6.5 0.0 all-gather.2.cloned.1.call-start
  6.5 0.7 all-gather.2.cloned.1.call-update
  7.3 0.0 copy-start.1
  7.3 0.0 copy-start.2
  7.3 0.0 all-reduce.2.cloned.1.call-start
  7.3 179.8 %all-gather.2.cloned.1.call-done = bf16[448,16384]{1,0:T(8,128)(2,1)} async-done(((bf16[224,16384]{1,0:T(8,128)(2,1)}), bf16[448,16384]{1,0:T(8,128)(2,1)}) %all-gather.2.cloned.1.call-update) | async-done | bytes 14680080 | tf_op jit(solution)/shard_map/all_gather | solution.py:16
  187.2 16.5 %fusion = f32[448,512]{1,0:T(8,128)} fusion(bf16[448,16384]{1,0:T(8,128)(2,1)} %all-gather.2.cloned.1.call-done, bf16[16384,512]{1,0:T(8,128)(2,1)} %param.6), kind=kOutput, calls=%fused_computation.4 | convolution fusion | flops 7516192768 | bytes 32374784 | tf_op jit(solution)/shard_map/dot_general | solution.py:15
  203.7 0.0 all-reduce.2.cloned.1.call-update
  203.7 0.0 copy-done.1
  203.7 0.1 dynamic-slice_add_fusion
  203.8 92.3 %all-reduce.2.cloned.1.call-done = f32[448,512]{1,0:T(8,128)} async-done(((f32[448,512]{1,0:T(8,128)}), f32[448,512]{1,0:T(8,128)}) %all-reduce.2.cloned.1.call-update) | async-done | bytes 917520 | tf_op jit(solution)/shard_map/psum | solution.py:20
  296.1 1.3 divide_convert_fusion
  297.4 13.2 %all_gather.7 = bf16[448,1024]{1,0:T(8,128)(2,1)S(1)} all-gather(bf16[448,512]{1,0:T(8,128)(2,1)S(1)} %divide_convert_fusion), channel_id=1, replica_groups=mesh['rows'=2,'feat'=16] {'rows'}, dimensions={1}, use_global_device_ids=true | all-gather | bytes 1376256 | tf_op jit(solution)/shard_map/all_gather | solution.py:25
  310.7 0.0 copy-done
  310.7 0.0 copy-done.2
  310.7 1.6 convolution_select_fusion
  (1 shorter events, 0.0 us)
Async XLA Ops:
  6.5 304.1 %copy-start = (bf16[512,1024]{1,0:T(8,128)(2,1)S(1)}, bf16[512,1024]{1,0:T(8,128)(2,1)}, u32[]{:S(2)}) copy-start(bf16[512,1024]{1,0:T(8,128)(2,1)} %param.8) | copy-start | bytes 3145732
  6.5 180.6 %all-gather.2.cloned.1.call-start = ((), (), s32[]{:S(2)}) async-start(), calls=%async_computation | async-start | bytes 22020096 | tf_op jit(solution)/shard_map/all_gather | solution.py:16
  7.3 196.5 %copy-start.1 = (f32[1024]{0:T(1024)S(1)}, f32[1024]{0:T(1024)}, u32[]{:S(2)}) copy-start(f32[1024]{0:T(1024)} %param.7) | copy-start | bytes 12292
  7.3 303.4 %copy-start.2 = (s32[448]{0:T(512)S(1)}, s32[448]{0:T(512)}, u32[]{:S(2)}) copy-start(s32[448]{0:T(512)} %param.9) | copy-start | bytes 5380
  7.3 288.9 %all-reduce.2.cloned.1.call-start = ((), (), s32[]{:S(2)}) async-start(), calls=%async_computation.1 | async-start | bytes 1835008 | tf_op jit(solution)/shard_map/psum | solution.py:20
Sparse Core Ops, SparseCore 0:
  8.9 178.2 all-gather.1
  203.8 92.2 all-reduce.1
where the time goes:
time: 319 us
  waiting for transfers between devices  273 us (86%)
  matrix products  18.1 us (6%)
  between operations  13.4 us (4%)
  blocking collectives  13.2 us (4%)
    all_gather x1, waiting for transfers between devices, shards(): lax.all_gather(slab_grads, 'rows', axis=0, tiled=True)  180 us
    psum x1, waiting for transfers between devices, shards(): summed = lax.psum(partial_value, 'feat')  92.3 us
    dot_general x1, matrix products, shards(): jnp.dot(lax.all_gather(slab_grads, 'rows', axis=0, tiled=True), basis, pr...  16.5 us
    all_gather x1, blocking collectives, shards(): gathered = lax.all_gather(whitened, 'rows', axis=1, tiled=True)  13.2 us
  transfers between devices with their start and end apart: 2, of which 2 were waited for; matrix products, arithmetic and copies ran while one was open for 0% of the time, Pallas kernels for 0%

commit v1 on v0

--- a/solution.py
+++ b/solution.py
@@ -17,7 +17,7 @@
         basis,
         preferred_element_type=jnp.float32,
     )
-    summed = lax.psum(partial_value, "feat")
+    summed = jnp.sum(lax.all_gather(partial_value, "feat"), axis=0)
     scales = lax.dynamic_slice_in_dim(
         eigenvalues, lax.axis_index("rows") * local_dirs, local_dirs, 0
     )

time: 319 us -> 346 us (1.085)
  waiting for transfers between devices: 273 us -> 294 us
  other arithmetic: 1.36 us -> 7.26 us
    all_gather x0 -> x1, waiting for transfers between devices: none -> 113 us  [shards(): summed = jnp.sum(lax.all_gather(partial_value, 'feat'), axis=0)]
    psum x1 -> x0, waiting for transfers between devices: 92.3 us -> none  [shards(): summed = lax.psum(partial_value, 'feat')]
    reduce_sum x0 -> x1, other arithmetic: none -> 7.07 us  [shards(): summed = jnp.sum(lax.all_gather(partial_value, 'feat'), axis=0)]
where the time goes in v1:
time: 346 us
  waiting for transfers between devices  294 us (85%)
  matrix products  18.1 us (5%)
  between operations  13.4 us (4%)
  blocking collectives  13.3 us (4%)
  other arithmetic  7.26 us (2%)
    all_gather x1, waiting for transfers between devices, shards(): lax.all_gather(slab_grads, 'rows', axis=0, tiled=True)  180 us
    all_gather x1, waiting for transfers between devices, shards(): summed = jnp.sum(lax.all_gather(partial_value, 'feat'), axis=0)  113 us
    dot_general x1, matrix products, shards(): jnp.dot(lax.all_gather(slab_grads, 'rows', axis=0, tiled=True), basis, pr...  16.5 us
    all_gather x1, blocking collectives, shards(): gathered = lax.all_gather(whitened, 'rows', axis=1, tiled=True)  13.3 us
    reduce_sum x1, other arithmetic, shards(): summed = jnp.sum(lax.all_gather(partial_value, 'feat'), axis=0)  7.07 us
  transfers between devices with their start and end apart: 2, of which 2 were waited for; matrix products, arithmetic and copies ran while one was open for 0% of the time, Pallas kernels for 0%

profile of v1, /device:TPU:0, one launch (start us, length us, event | category | flops | bytes accessed | tf_op | source)
XLA Modules:
  0.0 346.2 jit_solution(12851687484744743087)
XLA Ops:
  6.5 0.0 copy-start
  6.5 0.0 all-gather.4.cloned.1.call-start
  6.5 0.7 all-gather.4.cloned.1.call-update
  7.3 0.0 copy-start.1
  7.3 0.0 all-gather.6.cloned.1.call-start
  7.3 179.8 %all-gather.4.cloned.1.call-done = bf16[448,16384]{1,0:T(8,128)(2,1)} async-done(((bf16[224,16384]{1,0:T(8,128)(2,1)}), bf16[448,16384]{1,0:T(8,128)(2,1)}) %all-gather.4.cloned.1.call-update) | async-done | bytes 14680080 | tf_op jit(solution)/shard_map/all_gather | solution.py:16
  187.2 16.5 %fusion = f32[448,512]{1,0:T(8,128)} fusion(bf16[448,16384]{1,0:T(8,128)(2,1)} %all-gather.4.cloned.1.call-done, bf16[16384,512]{1,0:T(8,128)(2,1)} %param.6), kind=kOutput, calls=%fused_computation.4 | convolution fusion | flops 7516192768 | bytes 32374784 | tf_op jit(solution)/shard_map/dot_general | solution.py:15
  203.7 0.0 copy-start.2
  203.7 0.0 all-gather.6.cloned.1.call-update
  203.7 0.0 copy-done.1
  203.7 0.1 dynamic-slice_add_fusion
  203.8 113.4 %all-gather.6.cloned.1.call-done = f32[7168,512]{1,0:T(8,128)} async-done(((f32[448,512]{1,0:T(8,128)}), f32[7168,512]{1,0:T(8,128)}) %all-gather.6.cloned.1.call-update) | async-done | bytes 14680080 | tf_op jit(solution)/shard_map/all_gather | solution.py:20
  317.2 7.1 %reduce_sum.9 = f32[448,512]{1,0:T(8,128)S(1)} reduce(f32[16,448,512]{2,1,0:T(8,128)} %bitcast.5, f32[]{:T(128)} %constant.7.clone.1), dimensions={0}, to_apply=%region_0.0 | reduce | flops 3440640 | bytes 15597572 | tf_op jit(solution)/shard_map/reduce_sum | solution.py:20
  324.3 0.1 divide_convert_fusion
  324.4 13.3 %all_gather.15 = bf16[448,1024]{1,0:T(8,128)(2,1)S(1)} all-gather(bf16[448,512]{1,0:T(8,128)(2,1)S(1)} %divide_convert_fusion), channel_id=1, replica_groups=mesh['rows'=2,'feat'=16] {'rows'}, dimensions={1}, use_global_device_ids=true | all-gather | bytes 1376256 | tf_op jit(solution)/shard_map/all_gather | solution.py:25
  337.7 0.0 copy-done
  337.7 0.0 copy-done.2
  337.7 1.6 convolution_select_fusion
  (1 shorter events, 0.0 us)
Async XLA Ops:
  6.5 331.2 %copy-start = (bf16[512,1024]{1,0:T(8,128)(2,1)S(1)}, bf16[512,1024]{1,0:T(8,128)(2,1)}, u32[]{:S(2)}) copy-start(bf16[512,1024]{1,0:T(8,128)(2,1)} %param.8) | copy-start | bytes 3145732
  6.5 180.6 %all-gather.4.cloned.1.call-start = ((), (), s32[]{:S(2)}) async-start(), calls=%async_computation | async-start | bytes 22020096 | tf_op jit(solution)/shard_map/all_gather | solution.py:16
  7.3 196.5 %copy-start.1 = (f32[1024]{0:T(1024)S(1)}, f32[1024]{0:T(1024)}, u32[]{:S(2)}) copy-start(f32[1024]{0:T(1024)} %param.7) | copy-start | bytes 12292
  7.3 309.9 %all-gather.6.cloned.1.call-start = ((), (), s32[]{:S(2)}) async-start(), calls=%async_computation.1 | async-start | bytes 15597568 | tf_op jit(solution)/shard_map/all_gather | solution.py:20
  203.7 134.1 %copy-start.2 = (s32[448]{0:T(512)S(1)}, s32[448]{0:T(512)}, u32[]{:S(2)}) copy-start(s32[448]{0:T(512)} %param.9) | copy-start | bytes 5380
Sparse Core Ops, SparseCore 0:
  8.9 178.2 all-gather.3
  203.8 113.3 all-gather.5

commit v2 on v0

--- a/solution.py
+++ b/solution.py
@@ -13,7 +13,9 @@
     columns = first_column + jnp.arange(store_count, dtype=jnp.int32)
     local_dirs = basis.shape[1]
     partial_value = jnp.dot(
-        lax.all_gather(slab_grads, "rows", axis=0, tiled=True),
+        jnp.concatenate(
+            lax.all_to_all(jnp.stack([slab_grads] * lax.axis_size("rows")), "rows", 0, 0), axis=0
+        ),
         basis,
         preferred_element_type=jnp.float32,
     )

time: 319 us -> 308 us (0.966)
  waiting for transfers between devices: 273 us -> 92.8 us
  blocking collectives: 13.2 us -> 178 us
  other arithmetic: 1.36 us -> 10.4 us
  matrix products: 18.1 us -> 13.2 us
    all_gather x1 -> x0, waiting for transfers between devices: 180 us -> none  [shards(): lax.all_gather(slab_grads, 'rows', axis=0, tiled=True)]
    all_to_all x0 -> x1, blocking collectives: none -> 165 us  [shards(): lax.all_to_all(jnp.stack([slab_grads] * lax.axis_size('rows')), 'rows', 0...]
    another operation x0 -> x1, other arithmetic: none -> 9.04 us  [shards(): jnp.stack([slab_grads] * lax.axis_size('rows'))]
    dot_general x1, matrix products: 16.5 us -> 11.5 us  [shards(): jnp.dot(jnp.concatenate(lax.all_to_all(jnp.stack([slab_grads] * lax.axis_...]
  transfers between devices with their start and end apart: 2 -> 1, of which waited for: 2 -> 1; matrix products, arithmetic and copies ran while one was open for 0% -> 0% of each run, Pallas kernels for 0% -> 0%
where the time goes in v2:
time: 308 us
  blocking collectives  178 us (58%)
  waiting for transfers between devices  92.8 us (30%)
  between operations  13.4 us (4%)
  matrix products  13.2 us (4%)
  other arithmetic  10.4 us (3%)
    all_to_all x1, blocking collectives, shards(): lax.all_to_all(jnp.stack([slab_grads] * lax.axis_size('rows')), 'rows', 0...  165 us
    psum x1, waiting for transfers between devices, shards(): summed = lax.psum(partial_value, 'feat')  92.8 us
    all_gather x1, blocking collectives, shards(): gathered = lax.all_gather(whitened, 'rows', axis=1, tiled=True)  13.2 us
    dot_general x1, matrix products, shards(): jnp.dot(jnp.concatenate(lax.all_to_all(jnp.stack([slab_grads] * lax.axis_...  11.5 us
    another operation x1, other arithmetic, shards(): jnp.stack([slab_grads] * lax.axis_size('rows'))  9.04 us
  transfers between devices with their start and end apart: 1, of which 1 were waited for; matrix products, arithmetic and copies ran while one was open for 0% of the time, Pallas kernels for 0%

profile of v2, /device:TPU:0, one launch (start us, length us, event | category | flops | bytes accessed | tf_op | source)
XLA Modules:
  0.0 307.9 jit_solution(6555375980799515568)
XLA Ops:
  6.5 0.0 copy-start
  6.5 0.0 all-reduce.2.cloned.1.call-start
  6.5 9.0 %pad_maximum_fusion = bf16[2,224,16384]{2,1,0:T(8,128)(2,1)S(1)} fusion(bf16[1,224,16384]{2,1,0:T(8,128)(2,1)} %bitcast.7), kind=kLoop, calls=%fused_computation | loop fusion | flops 7340032 | bytes 22020096 | tf_op jit(solution)/shard_map/stack | solution.py:17
  15.6 164.8 %all_to_all.5 = bf16[2,224,16384]{2,1,0:T(8,128)(2,1)S(1)} all-to-all(bf16[2,224,16384]{2,1,0:T(8,128)(2,1)S(1)} %pad_maximum_fusion), channel_id=1, replica_groups=mesh['rows'=2,'feat'=16] {'rows'}, dimensions={0} | all-to-all | bytes 29360128 | tf_op jit(solution)/shard_map/all_to_all | solution.py:17
  180.4 0.0 copy-start.1
  180.4 0.0 copy-start.2
  180.4 11.5 %fusion = f32[448,512]{1,0:T(8,128)} fusion(bf16[448,16384]{1,0:T(8,128)(2,1)S(1)} %bitcast.6, bf16[16384,512]{1,0:T(8,128)(2,1)} %param.6), kind=kOutput, calls=%fused_computation.5 | convolution fusion | flops 7516192768 | bytes 32374784 | tf_op jit(solution)/shard_map/dot_general | solution.py:15
  191.9 0.0 all-reduce.2.cloned.1.call-update
  192.0 0.0 copy-done.1
  192.0 0.1 dynamic-slice_add_fusion
  192.1 92.8 %all-reduce.2.cloned.1.call-done = f32[448,512]{1,0:T(8,128)} async-done(((f32[448,512]{1,0:T(8,128)}), f32[448,512]{1,0:T(8,128)}) %all-reduce.2.cloned.1.call-update) | async-done | bytes 917520 | tf_op jit(solution)/shard_map/psum | solution.py:22
  284.9 1.3 divide_convert_fusion
  286.2 13.2 %all_gather.3 = bf16[448,1024]{1,0:T(8,128)(2,1)S(1)} all-gather(bf16[448,512]{1,0:T(8,128)(2,1)S(1)} %divide_convert_fusion), channel_id=1, replica_groups=mesh['rows'=2,'feat'=16] {'rows'}, dimensions={1}, use_global_device_ids=true | all-gather | bytes 1376256 | tf_op jit(solution)/shard_map/all_gather | solution.py:27
  299.4 0.0 copy-done
  299.4 0.0 copy-done.2
  299.4 1.6 convolution_select_fusion
  (1 shorter events, 0.0 us)
Async XLA Ops:
  6.5 292.9 %copy-start = (bf16[512,1024]{1,0:T(8,128)(2,1)S(1)}, bf16[512,1024]{1,0:T(8,128)(2,1)}, u32[]{:S(2)}) copy-start(bf16[512,1024]{1,0:T(8,128)(2,1)} %param.8) | copy-start | bytes 3145732
  6.5 278.3 %all-reduce.2.cloned.1.call-start = ((), (), s32[]{:S(2)}) async-start(), calls=%async_computation.1 | async-start | bytes 1835008 | tf_op jit(solution)/shard_map/psum | solution.py:22
  180.4 11.6 %copy-start.1 = (f32[1024]{0:T(1024)S(1)}, f32[1024]{0:T(1024)}, u32[]{:S(2)}) copy-start(f32[1024]{0:T(1024)} %param.7) | copy-start | bytes 12292
  180.4 119.0 %copy-start.2 = (s32[448]{0:T(512)S(1)}, s32[448]{0:T(512)}, u32[]{:S(2)}) copy-start(s32[448]{0:T(512)} %param.9) | copy-start | bytes 5380
Sparse Core Ops, SparseCore 0:
  192.1 92.7 all-reduce.1
